TPU v7x, 32 devices: a whole 2x2x4 slice. The times are simulated.
32 devices in a mesh: dp: 4 (over y, x), expert: 8 (over z, core).
Axes of the slice: x: 2, y: 2, z: 4, core: 2. Of those that a mesh axis runs over, the one named last changes fastest.
Arguments:
- tokens: bfloat16 [256, 3584], P('expert', 'dp'), may hold values from -6 to 6
- upstream: bfloat16 [256, 3584], P('expert', 'dp'), may hold values from -6 to 6
- expert_ids: int32 [256, 8], P('expert'), may hold values from 0 to 31, all different within a row
- gates: float32 [256, 8], P('expert'), may hold values from 0.2 to 1
- hot: int32 [8], replicated, may hold values from 0 to 1, as said below
- w_in: bfloat16 [8, 3584, 2048], P('expert', 'dp'), may hold values from -0.09375 to 0.09375
- w_down: bfloat16 [8, 1024, 3584], P('expert', None, 'dp'), may hold values from -0.1875 to 0.1875
Outputs:
- layer_out: bfloat16 [256, 3584], P('expert', 'dp')
- token_grad: bfloat16 [256, 3584], P('expert', 'dp')
- grad_in: bfloat16 [8, 3584, 2048], P('expert', 'dp')
- grad_down: bfloat16 [8, 1024, 3584], P('expert', None, 'dp')
Inputs may be any that keep to these rules, and one draw needn't show every extreme that they name: `expert_ids`: each row names 8 different experts; only those below 8 are computed by this layer. Every expert below 4 is hot; the others may or may not be.
All inputs are finite; a program needn't handle non-finite values.
Results may differ from a plain program's by a relative error of at most 0.028.
Values may be sent and summed in bfloat16 or wider, within the bound.
No kernel may reach another device: no remote copies, remote signals or barrier semaphores. Data moves between devices by JAX's collectives and lax.ppermute only.
A program may use at most 64 MiB of HBM per device.

v0:
```python
import jax
import jax.numpy as jnp
from jax import lax
from jax.sharding import PartitionSpec as P

CAP = 2


def plan_block(flat_ids, hot, expert_count, capacity):
    expert_lane = jnp.arange(expert_count, dtype=jnp.int32)
    in_window = flat_ids < expert_count
    chosen = ((flat_ids[:, None] == expert_lane[None, :]) & in_window[:, None]).astype(jnp.int32)
    occurrence = jnp.sum((jnp.cumsum(chosen, axis=0) - chosen) * chosen, axis=1)
    marked = jnp.sum(chosen * hot[None, :], axis=1)
    replica = (marked > 0) & (occurrence % 2 == 1)
    expert = jnp.where(in_window, flat_ids, 0)
    host_column = jnp.where(replica, (expert + expert_count // 2) % expert_count, expert)
    region_key = host_column + replica.astype(jnp.int32) * expert_count
    key_lane = jnp.arange(2 * expert_count, dtype=jnp.int32)
    keyed = ((region_key[:, None] == key_lane[None, :]) & in_window[:, None]).astype(jnp.int32)
    slot_rank = jnp.sum((jnp.cumsum(keyed, axis=0) - keyed) * keyed, axis=1)
    retained = in_window & (slot_rank < capacity)
    return (expert, host_column, slot_rank, replica, retained)


def fill_slots(position, total_slots):
    counts = position.shape[0]
    slot_index = jnp.full((total_slots + 1,), counts, jnp.int32)
    slot_index = slot_index.at[position].set(jnp.arange(counts, dtype=jnp.int32))
    return slot_index[:total_slots]


def pack_rows(slot_index, tokens, upstream, flat_gates, top_count):
    counts = flat_gates.shape[0]
    usable = slot_index < counts
    safe_index = jnp.where(usable, slot_index, 0)
    token_row = safe_index // top_count
    rows_in = jnp.where(usable[:, None], tokens[token_row], jnp.zeros((), jnp.bfloat16))
    scaled = flat_gates[safe_index][:, None] * upstream[token_row].astype(jnp.float32)
    rows_grad = jnp.where(usable[:, None], scaled, 0.0).astype(jnp.bfloat16)
    return (rows_in, rows_grad)


def activate(projected):
    half_width = projected.shape[1] // 2
    gate_part = projected[:, :half_width]
    up_part = projected[:, half_width:]
    sigmoid_gate = jax.nn.sigmoid(gate_part)
    hidden = (gate_part * sigmoid_gate * up_part).astype(jnp.bfloat16)
    return (gate_part, up_part, sigmoid_gate, hidden)


def pair_grads(hidden_grad, gate_part, up_part, sigmoid_gate):
    gate_grad = hidden_grad * up_part * sigmoid_gate * (1.0 + gate_part * (1.0 - sigmoid_gate))
    up_grad = hidden_grad * gate_part * sigmoid_gate
    return jnp.concatenate([gate_grad, up_grad], axis=1).astype(jnp.bfloat16)


def contract_last(left, right):
    return lax.dot_general(
        left, right, (((1,), (1,)), ((), ())), preferred_element_type=jnp.float32
    )


def contract_first(left, right):
    return lax.dot_general(
        left, right, (((0,), (0,)), ((), ())), preferred_element_type=jnp.float32
    )


def body(tokens, upstream, expert_ids, gates, hot, w_in, w_down):
    expert_count = hot.shape[0]
    token_count, top_count = expert_ids.shape
    share = tokens.shape[1]
    region_slots = expert_count * CAP
    total_slots = 2 * region_slots
    flat_gates = gates.reshape(-1)
    expert, host_column, slot_rank, replica, retained = plan_block(
        expert_ids.reshape(-1), hot, expert_count, CAP
    )
    own_in = w_in[0]
    own_down = w_down[0]
    far_in, far_down = (own_in, own_down)
    position = jnp.where(
        retained, expert * (2 * CAP) + replica.astype(jnp.int32) * CAP + slot_rank, total_slots
    )
    rows_in, rows_grad = pack_rows(
        fill_slots(position, total_slots), tokens, upstream, flat_gates, top_count
    )
    sent = (
        lax.all_to_all(
            rows_in.reshape(expert_count, 2, CAP, share),
            "expert",
            split_axis=0,
            concat_axis=0,
            tiled=True,
        ),
        lax.all_to_all(
            rows_grad.reshape(expert_count, 2, CAP, share),
            "expert",
            split_axis=0,
            concat_axis=0,
            tiled=True,
        ),
    )
    near_rows = sent[0][:, 0].reshape(region_slots, share)
    far_rows = sent[0][:, 1].reshape(region_slots, share)
    near_grad = sent[1][:, 0].reshape(region_slots, share)
    far_grad = sent[1][:, 1].reshape(region_slots, share)
    proj_part = jnp.concatenate(
        [
            jnp.dot(near_rows, own_in, preferred_element_type=jnp.float32),
            jnp.dot(far_rows, far_in, preferred_element_type=jnp.float32),
        ],
        axis=0,
    )
    grad_part = jnp.concatenate(
        [contract_last(near_grad, own_down), contract_last(far_grad, far_down)], axis=0
    )
    projected, hidden_grad = (
        lax.psum(proj_part.astype(jnp.bfloat16), "dp").astype(jnp.float32),
        lax.psum(grad_part.astype(jnp.bfloat16), "dp").astype(jnp.float32),
    )
    gate_part, up_part, sigmoid_gate, hidden = activate(projected)
    pair_grad = pair_grads(hidden_grad, gate_part, up_part, sigmoid_gate)
    near_hidden = hidden[:region_slots]
    far_hidden = hidden[region_slots:]
    near_pair = pair_grad[:region_slots]
    far_pair = pair_grad[region_slots:]
    out_near = jnp.dot(near_hidden, own_down, preferred_element_type=jnp.float32).astype(
        jnp.bfloat16
    )
    out_far = jnp.dot(far_hidden, far_down, preferred_element_type=jnp.float32).astype(jnp.bfloat16)
    input_near = contract_last(near_pair, own_in).astype(jnp.bfloat16)
    input_far = contract_last(far_pair, far_in).astype(jnp.bfloat16)
    near_in_grad = contract_first(near_rows, near_pair)
    near_down_grad = contract_first(near_hidden, near_grad)
    far_in_grad = contract_first(far_rows, far_pair).astype(jnp.bfloat16)
    far_down_grad = contract_first(far_hidden, far_grad).astype(jnp.bfloat16)
    back_in, back_down = lax.optimization_barrier((far_in_grad, far_down_grad))
    grad_in = (near_in_grad + back_in.astype(jnp.float32)).astype(jnp.bfloat16)
    grad_down = (near_down_grad + back_down.astype(jnp.float32)).astype(jnp.bfloat16)
    out_rows = jnp.stack(
        [out_near.reshape(expert_count, CAP, share), out_far.reshape(expert_count, CAP, share)],
        axis=1,
    )
    input_rows = jnp.stack(
        [input_near.reshape(expert_count, CAP, share), input_far.reshape(expert_count, CAP, share)],
        axis=1,
    )
    back = (
        lax.all_to_all(out_rows, "expert", split_axis=0, concat_axis=0, tiled=True),
        lax.all_to_all(input_rows, "expert", split_axis=0, concat_axis=0, tiled=True),
    )
    returned_out = back[0].reshape(total_slots, share)
    returned_input = back[1].reshape(total_slots, share)
    safe_lookup = jnp.where(retained, position, 0)
    picked_out = jnp.where(retained[:, None], returned_out[safe_lookup].astype(jnp.float32), 0.0)
    picked_input = jnp.where(
        retained[:, None], returned_input[safe_lookup].astype(jnp.float32), 0.0
    )
    weighted = (picked_out * flat_gates[:, None]).reshape(token_count, top_count, share)
    layer_out = jnp.sum(weighted, axis=1).astype(jnp.bfloat16)
    token_grad = jnp.sum(picked_input.reshape(token_count, top_count, share), axis=1).astype(
        jnp.bfloat16
    )
    return (layer_out, token_grad, grad_in[None], grad_down[None])


def solution(mesh):
    return jax.shard_map(
        body,
        mesh=mesh,
        in_specs=(
            P("expert", "dp"),
            P("expert", "dp"),
            P("expert", None),
            P("expert", None),
            P(),
            P("expert", "dp", None),
            P("expert", None, "dp"),
        ),
        out_specs=(
            P("expert", "dp"),
            P("expert", "dp"),
            P("expert", "dp", None),
            P("expert", None, "dp"),
        ),
        check_vma=False,
    )
```

profile of v0, /device:TPU:0, one launch (start us, length us, event | category | flops | bytes accessed | tf_op | source)
XLA Modules:
  0.0 121.8 jit_solution(12306745262388308910)
XLA Ops:
  7.2 0.9 copy.24
  9.2 0.8 select_reduce_fusion
  11.0 1.4 %scatter_custom_fusion = s32[33]{0:T(128)S(1)} fusion(s32[256]{0:T(256)S(1)} %bitcast.102, s32[256]{0:T(256)S(1)} %iota.19, s32[]{:T(128)} %constant.64.clone.1), kind=kCustom, calls=%fused_computation.135 | custom fusion | bytes 136 | tf_op jit(solution)/shard_map/scatter | solution.py:29
  12.4 1.5 %gather_fusion = bf16[32,896]{1,0:T(8,128)(2,1)S(1)} fusion(bf16[32,896]{1,0:T(8,128)(2,1)} %param.7, s32[1024]{0:T(1024)S(1)} %get-tuple-element.28), kind=kCustom, calls=%fused_computation | custom fusion | bytes 114816 | tf_op jit(solution)/shard_map/gather | solution.py:38
  14.1 0.8 broadcast_select_fusion
  14.8 6.4 %all-to-all-start = ((bf16[8,2,2,896]{3,2,1,0:T(2,128)(2,1)}), bf16[8,2,2,896]{3,2,1,0:T(2,128)(2,1)S(1)}, u32[]{:S(2)}, u32[]{:S(2)}) async-start(bf16[8,2,2,896]{3,2,1,0:T(2,128)(2,1)} %broadcast_select_fusion), calls=%async_computation | async-start | bytes 114688 | tf_op jit(solution)/shard_map/all_to_all | solution.py:91
  21.2 1.5 %gather_fusion.3 = bf16[32,896]{1,0:T(8,128)(2,1)S(1)} fusion(bf16[32,896]{1,0:T(8,128)(2,1)} %param.8, s32[1024]{0:T(1024)S(1)} %get-tuple-element.28), kind=kCustom, calls=%fused_computation.3 | custom fusion | bytes 114816 | tf_op jit(solution)/shard_map/gather | solution.py:39
  22.8 0.8 copy.31
  23.6 0.7 gather_fusion.2
  24.5 0.8 select_convert_fusion
  25.3 1.8 %all-to-all-done = bf16[8,2,2,896]{3,2,1,0:T(2,128)(2,1)S(1)} async-done(((bf16[8,2,2,896]{3,2,1,0:T(2,128)(2,1)}), bf16[8,2,2,896]{3,2,1,0:T(2,128)(2,1)S(1)}, u32[]{:S(2)}, u32[]{:S(2)}) %all-to-all-start) | async-done | bytes 57376 | tf_op jit(solution)/shard_map/all_to_all | solution.py:91
  27.1 3.3 %all-to-all-start.2 = ((bf16[8,2,2,896]{3,2,1,0:T(2,128)(2,1)}), bf16[8,2,2,896]{3,2,1,0:T(2,128)(2,1)S(1)}, u32[]{:S(2)}, u32[]{:S(2)}) async-start(bf16[8,2,2,896]{3,2,1,0:T(2,128)(2,1)} %select_convert_fusion), calls=%async_computation.2 | async-start | bytes 114688 | tf_op jit(solution)/shard_map/all_to_all | solution.py:98
  30.6 2.8 %fusion.12 = bf16[16,2048]{1,0:T(8,128)(2,1)S(1)} fusion(bf16[16,896]{1,0:T(8,128)(2,1)S(1)} %reshape_squeeze.13, bf16[1,896,2048]{2,1,0:T(8,128)(2,1)} %param.12), kind=kOutput, calls=%fused_computation.19 | convolution fusion | flops 58753024 | bytes 3764224 | tf_op jit(solution)/shard_map/dot_general | solution.py:113
  34.3 2.0 %all-to-all-done.2 = bf16[8,2,2,896]{3,2,1,0:T(2,128)(2,1)S(1)} async-done(((bf16[8,2,2,896]{3,2,1,0:T(2,128)(2,1)}), bf16[8,2,2,896]{3,2,1,0:T(2,128)(2,1)S(1)}, u32[]{:S(2)}, u32[]{:S(2)}) %all-to-all-start.2) | async-done | bytes 57376 | tf_op jit(solution)/shard_map/all_to_all | solution.py:98
  38.9 42.2 %all-reduce.3.cloned.1.call-done = (bf16[32,1024]{1,0:T(8,128)(2,1)}, bf16[32,2048]{1,0:T(8,128)(2,1)}) async-done(((bf16[32,1024]{1,0:T(8,128)(2,1)}, bf16[32,2048]{1,0:T(8,128)(2,1)}), (bf16[32,1024]{1,0:T(8,128)(2,1)}, bf16[32,2048]{1,0:T(8,128)(2,1)})) %all-reduce.3.cloned.1.call-update) | async-done | bytes 196624 | tf_op jit(solution)/shard_map/psum | solution.py:122
  81.1 0.9 convert_element_type.93
  82.0 0.9 fusion.47
  82.9 1.9 %convolution_convert_fusion.1 = bf16[1024,896]{1,0:T(8,128)(2,1)} fusion(bf16[16,896]{1,0:T(8,128)(2,1)S(1)} %reshape_squeeze.15, bf16[32,1024]{1,0:T(8,128)(2,1)S(1)} %get-tuple-element.20), kind=kOutput, calls=%fused_computation.28 | convolution fusion | flops 30277632 | bytes 1896448 | tf_op jit(solution)/shard_map/dot_general | solution.py:66
  85.5 1.2 convolution_convert_fusion
  86.9 1.0 fusion.36
  87.9 1.1 fusion.39
  89.0 3.0 %fusion.8 = bf16[1,896,2048]{2,1,0:T(8,128)(2,1)} fusion(bf16[896,2048]{1,0:T(8,128)(2,1)S(1)} %convolution_convert_fusion, bf16[16,896]{1,0:T(8,128)(2,1)S(1)} %reshape_squeeze.12, bf16[32,1024]{1,0:T(8,128)(2,1)S(1)} %get-tuple-element.18, bf16[32,1024]{1,0:T(8,128)(2,1)S(1)} %get-tuple-element.19), kind=kOutput, calls=%fused_computation.17 | convolution fusion | flops 64356352 | bytes 7499776 | tf_op jit(solution)/shard_map/dot_general | solution.py:66
  92.0 0.7 pad_maximum_fusion.3
  92.7 4.6 %all-to-all-start.1 = ((bf16[8,2,2,896]{3,2,1,0:T(2,128)(2,1)}), bf16[8,2,2,896]{3,2,1,0:T(2,128)(2,1)S(1)}, u32[]{:S(2)}, u32[]{:S(2)}) async-start(bf16[8,2,2,896]{3,2,1,0:T(2,128)(2,1)} %pad_maximum_fusion.3), calls=%async_computation.1 | async-start | bytes 114688 | tf_op jit(solution)/shard_map/all_to_all | solution.py:152
  97.4 0.7 pad_maximum_fusion.4
  98.1 5.1 %all-to-all-done.1 = bf16[8,2,2,896]{3,2,1,0:T(2,128)(2,1)S(1)} async-done(((bf16[8,2,2,896]{3,2,1,0:T(2,128)(2,1)}), bf16[8,2,2,896]{3,2,1,0:T(2,128)(2,1)S(1)}, u32[]{:S(2)}, u32[]{:S(2)}) %all-to-all-start.1) | async-done | bytes 57376 | tf_op jit(solution)/shard_map/all_to_all | solution.py:152
  103.2 3.5 %all-to-all-start.3 = ((bf16[8,2,2,896]{3,2,1,0:T(2,128)(2,1)}), bf16[8,2,2,896]{3,2,1,0:T(2,128)(2,1)S(1)}, u32[]{:S(2)}, u32[]{:S(2)}) async-start(bf16[8,2,2,896]{3,2,1,0:T(2,128)(2,1)} %pad_maximum_fusion.4), calls=%async_computation.3 | async-start | bytes 114688 | tf_op jit(solution)/shard_map/all_to_all | solution.py:153
  106.8 3.4 %fusion.23 = bf16[1,1024,896]{2,1,0:T(8,128)(2,1)} fusion(bf16[1024,896]{1,0:T(8,128)(2,1)} %convolution_convert_fusion.1, bf16[16,896]{1,0:T(8,128)(2,1)S(1)} %reshape_squeeze.14, bf16[32,1024]{1,0:T(8,128)(2,1)S(1)} %get-tuple-element.20), kind=kOutput, calls=%fused_computation.29 | convolution fusion | flops 32112640 | bytes 3731456 | tf_op jit(solution)/shard_map/dot_general | solution.py:66
  110.2 1.2 gather_fusion.1
  111.4 1.0 all-to-all-done.3
  112.4 1.2 gather_fusion.4
  113.6 1.3 %fusion.42 = (bf16[32,896]{1,0:T(8,128)(2,1)}, bf16[32,896]{1,0:T(8,128)(2,1)}) fusion(bf16[256,896]{1,0:T(8,128)(2,1)S(1)} %gather_fusion.4, pred[32,8]{1,0:T(8,128)(4,1)S(1)} %compare_and_fusion, f32[32,8]{1,0:T(8,128)S(1)} %copy.31, bf16[256,896]{1,0:T(8,128)(2,1)S(1)} %gather_fusion.1), kind=kLoop, calls=%fused_computation.37 | loop fusion | flops 1548288 | bytes 1033472 | tf_op jit(solution)/shard_map/reduce_sum | solution.py:164
  (60 shorter events, 7.2 us)
Async XLA Ops:
  7.2 29.2 %copy-start = (bf16[1,1024,896]{2,1,0:T(8,128)(2,1)S(1)}, bf16[1,1024,896]{2,1,0:T(8,128)(2,1)}, u32[]{:S(2)}) copy-start(bf16[1,1024,896]{2,1,0:T(8,128)(2,1)} %param.13) | copy-start | bytes 5505028
  14.8 12.2 %all-to-all-start = ((bf16[8,2,2,896]{3,2,1,0:T(2,128)(2,1)}), bf16[8,2,2,896]{3,2,1,0:T(2,128)(2,1)S(1)}, u32[]{:S(2)}, u32[]{:S(2)}) async-start(bf16[8,2,2,896]{3,2,1,0:T(2,128)(2,1)} %broadcast_select_fusion), calls=%async_computation | async-start | bytes 114688 | tf_op jit(solution)/shard_map/all_to_all | solution.py:91
  27.1 9.2 %all-to-all-start.2 = ((bf16[8,2,2,896]{3,2,1,0:T(2,128)(2,1)}), bf16[8,2,2,896]{3,2,1,0:T(2,128)(2,1)S(1)}, u32[]{:S(2)}, u32[]{:S(2)}) async-start(bf16[8,2,2,896]{3,2,1,0:T(2,128)(2,1)} %select_convert_fusion), calls=%async_computation.2 | async-start | bytes 114688 | tf_op jit(solution)/shard_map/all_to_all | solution.py:98
  30.4 50.7 %all-reduce.3.cloned.1.call-start = ((), (), s32[]{:S(2)}) async-start(), calls=%async_computation.4 | async-start | bytes 393216 | tf_op jit(solution)/shard_map/psum | solution.py:122
  30.6 3.1 %copy-start.1 = (bf16[1,896,2048]{2,1,0:T(8,128)(2,1)S(1)}, bf16[1,896,2048]{2,1,0:T(8,128)(2,1)}, u32[]{:S(2)}) copy-start(bf16[1,896,2048]{2,1,0:T(8,128)(2,1)} %param.12) | copy-start | bytes 11010052
  84.8 2.0 %copy-start.2 = (bf16[1,896,2048]{2,1,0:T(8,128)(2,1)S(1)}, bf16[1,896,2048]{2,1,0:T(8,128)(2,1)}, u32[]{:S(2)}) copy-start(bf16[1,896,2048]{2,1,0:T(8,128)(2,1)} %param.12) | copy-start | bytes 11010052
  92.7 10.5 %all-to-all-start.1 = ((bf16[8,2,2,896]{3,2,1,0:T(2,128)(2,1)}), bf16[8,2,2,896]{3,2,1,0:T(2,128)(2,1)S(1)}, u32[]{:S(2)}, u32[]{:S(2)}) async-start(bf16[8,2,2,896]{3,2,1,0:T(2,128)(2,1)} %pad_maximum_fusion.3), calls=%async_computation.1 | async-start | bytes 114688 | tf_op jit(solution)/shard_map/all_to_all | solution.py:152
  103.2 9.2 %all-to-all-start.3 = ((bf16[8,2,2,896]{3,2,1,0:T(2,128)(2,1)}), bf16[8,2,2,896]{3,2,1,0:T(2,128)(2,1)S(1)}, u32[]{:S(2)}, u32[]{:S(2)}) async-start(bf16[8,2,2,896]{3,2,1,0:T(2,128)(2,1)} %pad_maximum_fusion.4), calls=%async_computation.3 | async-start | bytes 114688 | tf_op jit(solution)/shard_map/all_to_all | solution.py:153
Sparse Core Ops, SparseCore 0:
  39.0 42.0 all-reduce.2
where the time goes:
time: 122 us
  waiting for transfers between devices  52.1 us (43%)
  starting transfers between devices  17.9 us (15%)
  matrix products  16.8 us (14%)
  between operations  14.3 us (12%)
  local copies, waits for them, and re-layouts  11.1 us (9%)
  other arithmetic  9.6 us (8%)
    psum x1, waiting for transfers between devices, body(): lax.psum(grad_part.astype(jnp.bfloat16), 'dp').astype(jnp.float32)  42.2 us
    dot_general x4, matrix products, contract_first(): lax.dot_general(left, right, (((0,), (0,)), ((), ())), preferred_element_...  9.47 us
    all_to_all x1, starting transfers between devices, body(): lax.all_to_all(rows_in.reshape(expert_count, 2, CAP, share), 'expert', sp...  6.35 us
    all_to_all x1, waiting for transfers between devices, body(): lax.all_to_all(out_rows, 'expert', split_axis=0, concat_axis=0, tiled=True)  5.13 us
    all_to_all x1, starting transfers between devices, body(): lax.all_to_all(out_rows, 'expert', split_axis=0, concat_axis=0, tiled=True)  4.6 us
    all_to_all x1, starting transfers between devices, body(): lax.all_to_all(input_rows, 'expert', split_axis=0, concat_axis=0, tiled=T...  3.53 us
    all_to_all x1, starting transfers between devices, body(): lax.all_to_all(rows_grad.reshape(expert_count, 2, CAP, share), 'expert',...  3.35 us
    dot_general x4, matrix products, contract_last(): lax.dot_general(left, right, (((1,), (1,)), ((), ())), preferred_element_...  3.28 us
  transfers between devices with their start and end apart: 5, of which 5 were waited for; matrix products, arithmetic and copies ran while one was open for 11% of the time, Pallas kernels for 0%

commit v1 on v0

--- a/solution.py
+++ b/solution.py
@@ -119,7 +119,7 @@
     )
     projected, hidden_grad = (
         lax.psum(proj_part.astype(jnp.bfloat16), "dp").astype(jnp.float32),
-        lax.psum(grad_part.astype(jnp.bfloat16), "dp").astype(jnp.float32),
+        jnp.sum(lax.all_gather(grad_part.astype(jnp.bfloat16), "dp"), axis=0).astype(jnp.float32),
     )
     gate_part, up_part, sigmoid_gate, hidden = activate(projected)
     pair_grad = pair_grads(hidden_grad, gate_part, up_part, sigmoid_gate)

time: 122 us -> 119 us (0.975)
  waiting for transfers between devices: 52.1 us -> 41.3 us
  blocking collectives: 0 us -> 9.04 us
  other arithmetic: 9.6 us -> 8.17 us
    psum x1, waiting for transfers between devices: 42.2 us -> 32.1 us  [body(): lax.psum(proj_part.astype(jnp.bfloat16), 'dp').astype(jnp.float32)]
    all_gather x0 -> x1, blocking collectives: none -> 9.04 us  [body(): lax.all_gather(grad_part.astype(jnp.bfloat16), 'dp')]
  transfers between devices with their start and end apart: 5 -> 5, of which waited for: 5 -> 5; matrix products, arithmetic and copies ran while one was open for 11% -> 13% of each run, Pallas kernels for 0% -> 0%
where the time goes in v1:
time: 119 us
  waiting for transfers between devices  41.3 us (35%)
  starting transfers between devices  17.9 us (15%)
  matrix products  16.8 us (14%)
  between operations  14.3 us (12%)
  local copies, waits for them, and re-layouts  11.1 us (9%)
  blocking collectives  9.04 us (8%)
  other arithmetic  8.17 us (7%)
    psum x1, waiting for transfers between devices, body(): lax.psum(proj_part.astype(jnp.bfloat16), 'dp').astype(jnp.float32)  32.1 us
    dot_general x4, matrix products, contract_first(): lax.dot_general(left, right, (((0,), (0,)), ((), ())), preferred_element_...  9.46 us
    all_gather x1, blocking collectives, body(): lax.all_gather(grad_part.astype(jnp.bfloat16), 'dp')  9.04 us
    all_to_all x1, starting transfers between devices, body(): lax.all_to_all(rows_in.reshape(expert_count, 2, CAP, share), 'expert', sp...  6.35 us
    all_to_all x1, waiting for transfers between devices, body(): lax.all_to_all(out_rows, 'expert', split_axis=0, concat_axis=0, tiled=True)  5.13 us
    all_to_all x1, starting transfers between devices, body(): lax.all_to_all(out_rows, 'expert', split_axis=0, concat_axis=0, tiled=True)  4.6 us
    all_to_all x1, starting transfers between devices, body(): lax.all_to_all(input_rows, 'expert', split_axis=0, concat_axis=0, tiled=T...  3.53 us
    all_to_all x1, starting transfers between devices, body(): lax.all_to_all(rows_grad.reshape(expert_count, 2, CAP, share), 'expert',...  3.35 us
  transfers between devices with their start and end apart: 5, of which 5 were waited for; matrix products, arithmetic and copies ran while one was open for 13% of the time, Pallas kernels for 0%

profile of v1, /device:TPU:0, one launch (start us, length us, event | category | flops | bytes accessed | tf_op | source)
XLA Modules:
  0.0 118.6 jit_solution(12167412400064172413)
XLA Ops:
  7.2 0.9 copy.24
  9.2 0.8 select_reduce_fusion
  11.0 1.4 %scatter_custom_fusion = s32[33]{0:T(128)S(1)} fusion(s32[256]{0:T(256)S(1)} %bitcast.110, s32[256]{0:T(256)S(1)} %iota.19, s32[]{:T(128)} %constant.65.clone.1), kind=kCustom, calls=%fused_computation.137 | custom fusion | bytes 136 | tf_op jit(solution)/shard_map/scatter | solution.py:29
  12.4 1.5 %gather_fusion = bf16[32,896]{1,0:T(8,128)(2,1)S(1)} fusion(bf16[32,896]{1,0:T(8,128)(2,1)} %param.7, s32[1024]{0:T(1024)S(1)} %get-tuple-element.26), kind=kCustom, calls=%fused_computation | custom fusion | bytes 114816 | tf_op jit(solution)/shard_map/gather | solution.py:38
  14.1 0.8 broadcast_select_fusion
  14.8 6.4 %all-to-all-start = ((bf16[8,2,2,896]{3,2,1,0:T(2,128)(2,1)}), bf16[8,2,2,896]{3,2,1,0:T(2,128)(2,1)S(1)}, u32[]{:S(2)}, u32[]{:S(2)}) async-start(bf16[8,2,2,896]{3,2,1,0:T(2,128)(2,1)} %broadcast_select_fusion), calls=%async_computation | async-start | bytes 114688 | tf_op jit(solution)/shard_map/all_to_all | solution.py:91
  21.2 1.5 %gather_fusion.3 = bf16[32,896]{1,0:T(8,128)(2,1)S(1)} fusion(bf16[32,896]{1,0:T(8,128)(2,1)} %param.8, s32[1024]{0:T(1024)S(1)} %get-tuple-element.26), kind=kCustom, calls=%fused_computation.3 | custom fusion | bytes 114816 | tf_op jit(solution)/shard_map/gather | solution.py:39
  22.8 0.8 copy.31
  23.6 0.7 gather_fusion.2
  24.5 0.8 select_convert_fusion
  25.3 1.8 %all-to-all-done = bf16[8,2,2,896]{3,2,1,0:T(2,128)(2,1)S(1)} async-done(((bf16[8,2,2,896]{3,2,1,0:T(2,128)(2,1)}), bf16[8,2,2,896]{3,2,1,0:T(2,128)(2,1)S(1)}, u32[]{:S(2)}, u32[]{:S(2)}) %all-to-all-start) | async-done | bytes 57376 | tf_op jit(solution)/shard_map/all_to_all | solution.py:91
  27.1 3.4 %all-to-all-start.2 = ((bf16[8,2,2,896]{3,2,1,0:T(2,128)(2,1)}), bf16[8,2,2,896]{3,2,1,0:T(2,128)(2,1)S(1)}, u32[]{:S(2)}, u32[]{:S(2)}) async-start(bf16[8,2,2,896]{3,2,1,0:T(2,128)(2,1)} %select_convert_fusion), calls=%async_computation.2 | async-start | bytes 114688 | tf_op jit(solution)/shard_map/all_to_all | solution.py:98
  30.6 2.8 %fusion.12 = bf16[16,2048]{1,0:T(8,128)(2,1)S(1)} fusion(bf16[16,896]{1,0:T(8,128)(2,1)S(1)} %reshape_squeeze.13, bf16[1,896,2048]{2,1,0:T(8,128)(2,1)} %param.12), kind=kOutput, calls=%fused_computation.19 | convolution fusion | flops 58753024 | bytes 3764224 | tf_op jit(solution)/shard_map/dot_general | solution.py:113
  35.0 1.3 %all-to-all-done.2 = bf16[8,2,2,896]{3,2,1,0:T(2,128)(2,1)S(1)} async-done(((bf16[8,2,2,896]{3,2,1,0:T(2,128)(2,1)}), bf16[8,2,2,896]{3,2,1,0:T(2,128)(2,1)S(1)}, u32[]{:S(2)}, u32[]{:S(2)}) %all-to-all-start.2) | async-done | bytes 57376 | tf_op jit(solution)/shard_map/all_to_all | solution.py:98
  37.6 9.0 %all_gather.4 = bf16[4,32,1024]{2,1,0:T(8,128)(2,1)S(1)} all-gather(bf16[1,32,1024]{2,1,0:T(8,128)(2,1)S(1)} %pad_maximum_fusion.2), channel_id=1, replica_groups=mesh['dp'=4,'expert'=8] {'dp'}, dimensions={0}, use_global_device_ids=true | all-gather | bytes 327680 | tf_op jit(solution)/shard_map/all_gather | solution.py:122
  46.7 32.1 %all-reduce.2.cloned.1.call-done = bf16[32,2048]{1,0:T(8,128)(2,1)} async-done(((bf16[32,2048]{1,0:T(8,128)(2,1)}), bf16[32,2048]{1,0:T(8,128)(2,1)}) %all-reduce.2.cloned.1.call-update) | async-done | bytes 131088 | tf_op jit(solution)/shard_map/psum | solution.py:121
  78.8 0.9 convert_element_type.102
  79.8 1.9 %convolution_convert_fusion.1 = bf16[1024,896]{1,0:T(8,128)(2,1)} fusion(bf16[16,896]{1,0:T(8,128)(2,1)S(1)} %reshape_squeeze.15, bf16[32,1024]{1,0:T(8,128)(2,1)S(1)} %get-tuple-element.18), kind=kOutput, calls=%fused_computation.28 | convolution fusion | flops 30277632 | bytes 1896448 | tf_op jit(solution)/shard_map/dot_general | solution.py:66
  82.4 1.2 convolution_convert_fusion
  83.7 1.0 fusion.36
  84.8 1.1 fusion.39
  85.8 3.0 %fusion.8 = bf16[1,896,2048]{2,1,0:T(8,128)(2,1)} fusion(bf16[896,2048]{1,0:T(8,128)(2,1)S(1)} %convolution_convert_fusion, bf16[16,896]{1,0:T(8,128)(2,1)S(1)} %reshape_squeeze.12, bf16[32,1024]{1,0:T(8,128)(2,1)S(1)} %get-tuple-element.16, bf16[32,1024]{1,0:T(8,128)(2,1)S(1)} %get-tuple-element.17), kind=kOutput, calls=%fused_computation.17 | convolution fusion | flops 64356352 | bytes 7499776 | tf_op jit(solution)/shard_map/dot_general | solution.py:66
  88.9 0.7 pad_maximum_fusion.3
  89.6 4.6 %all-to-all-start.1 = ((bf16[8,2,2,896]{3,2,1,0:T(2,128)(2,1)}), bf16[8,2,2,896]{3,2,1,0:T(2,128)(2,1)S(1)}, u32[]{:S(2)}, u32[]{:S(2)}) async-start(bf16[8,2,2,896]{3,2,1,0:T(2,128)(2,1)} %pad_maximum_fusion.3), calls=%async_computation.1 | async-start | bytes 114688 | tf_op jit(solution)/shard_map/all_to_all | solution.py:152
  94.2 0.7 pad_maximum_fusion.4
  94.9 5.1 %all-to-all-done.1 = bf16[8,2,2,896]{3,2,1,0:T(2,128)(2,1)S(1)} async-done(((bf16[8,2,2,896]{3,2,1,0:T(2,128)(2,1)}), bf16[8,2,2,896]{3,2,1,0:T(2,128)(2,1)S(1)}, u32[]{:S(2)}, u32[]{:S(2)}) %all-to-all-start.1) | async-done | bytes 57376 | tf_op jit(solution)/shard_map/all_to_all | solution.py:152
  100.1 3.5 %all-to-all-start.3 = ((bf16[8,2,2,896]{3,2,1,0:T(2,128)(2,1)}), bf16[8,2,2,896]{3,2,1,0:T(2,128)(2,1)S(1)}, u32[]{:S(2)}, u32[]{:S(2)}) async-start(bf16[8,2,2,896]{3,2,1,0:T(2,128)(2,1)} %pad_maximum_fusion.4), calls=%async_computation.3 | async-start | bytes 114688 | tf_op jit(solution)/shard_map/all_to_all | solution.py:153
  103.6 3.4 %fusion.23 = bf16[1,1024,896]{2,1,0:T(8,128)(2,1)} fusion(bf16[1024,896]{1,0:T(8,128)(2,1)} %convolution_convert_fusion.1, bf16[16,896]{1,0:T(8,128)(2,1)S(1)} %reshape_squeeze.14, bf16[32,1024]{1,0:T(8,128)(2,1)S(1)} %get-tuple-element.18), kind=kOutput, calls=%fused_computation.29 | convolution fusion | flops 32112640 | bytes 3731456 | tf_op jit(solution)/shard_map/dot_general | solution.py:66
  107.0 1.2 %gather_fusion.1 = bf16[256,896]{1,0:T(8,128)(2,1)S(1)} fusion(bf16[32,896]{1,0:T(8,128)(2,1)S(1)} %reshape.324, s32[1024]{0:T(1024)S(1)} %pad_clamp_fusion.1), kind=kCustom, calls=%fused_computation.1 | custom fusion | bytes 918528 | tf_op jit(solution)/shard_map/gather | solution.py:158
  108.2 1.0 all-to-all-done.3
  109.3 1.2 %gather_fusion.4 = bf16[256,896]{1,0:T(8,128)(2,1)S(1)} fusion(bf16[32,896]{1,0:T(8,128)(2,1)S(1)} %reshape.326, s32[1024]{0:T(1024)S(1)} %pad_clamp_fusion.1), kind=kCustom, calls=%fused_computation.4 | custom fusion | bytes 918528 | tf_op jit(solution)/shard_map/gather | solution.py:160
  110.5 1.3 %fusion.48 = (bf16[32,896]{1,0:T(8,128)(2,1)}, bf16[32,896]{1,0:T(8,128)(2,1)}) fusion(bf16[256,896]{1,0:T(8,128)(2,1)S(1)} %gather_fusion.4, pred[32,8]{1,0:T(8,128)(4,1)S(1)} %compare_and_fusion, f32[32,8]{1,0:T(8,128)S(1)} %copy.31, bf16[256,896]{1,0:T(8,128)(2,1)S(1)} %gather_fusion.1), kind=kLoop, calls=%fused_computation.39 | loop fusion | flops 1548288 | bytes 1033472 | tf_op jit(solution)/shard_map/reduce_sum | solution.py:164
  (62 shorter events, 6.8 us)
Async XLA Ops:
  7.2 29.2 %copy-start = (bf16[1,1024,896]{2,1,0:T(8,128)(2,1)S(1)}, bf16[1,1024,896]{2,1,0:T(8,128)(2,1)}, u32[]{:S(2)}) copy-start(bf16[1,1024,896]{2,1,0:T(8,128)(2,1)} %param.13) | copy-start | bytes 5505028
  14.8 12.2 %all-to-all-start = ((bf16[8,2,2,896]{3,2,1,0:T(2,128)(2,1)}), bf16[8,2,2,896]{3,2,1,0:T(2,128)(2,1)S(1)}, u32[]{:S(2)}, u32[]{:S(2)}) async-start(bf16[8,2,2,896]{3,2,1,0:T(2,128)(2,1)} %broadcast_select_fusion), calls=%async_computation | async-start | bytes 114688 | tf_op jit(solution)/shard_map/all_to_all | solution.py:91
  27.1 9.2 %all-to-all-start.2 = ((bf16[8,2,2,896]{3,2,1,0:T(2,128)(2,1)}), bf16[8,2,2,896]{3,2,1,0:T(2,128)(2,1)S(1)}, u32[]{:S(2)}, u32[]{:S(2)}) async-start(bf16[8,2,2,896]{3,2,1,0:T(2,128)(2,1)} %select_convert_fusion), calls=%async_computation.2 | async-start | bytes 114688 | tf_op jit(solution)/shard_map/all_to_all | solution.py:98
  30.4 48.4 %all-reduce.2.cloned.1.call-start = ((), (), s32[]{:S(2)}) async-start(), calls=%async_computation.4 | async-start | bytes 262144 | tf_op jit(solution)/shard_map/psum | solution.py:121
  30.6 3.1 %copy-start.1 = (bf16[1,896,2048]{2,1,0:T(8,128)(2,1)S(1)}, bf16[1,896,2048]{2,1,0:T(8,128)(2,1)}, u32[]{:S(2)}) copy-start(bf16[1,896,2048]{2,1,0:T(8,128)(2,1)} %param.12) | copy-start | bytes 11010052
  81.7 2.0 %copy-start.2 = (bf16[1,896,2048]{2,1,0:T(8,128)(2,1)S(1)}, bf16[1,896,2048]{2,1,0:T(8,128)(2,1)}, u32[]{:S(2)}) copy-start(bf16[1,896,2048]{2,1,0:T(8,128)(2,1)} %param.12) | copy-start | bytes 11010052
  89.6 10.5 %all-to-all-start.1 = ((bf16[8,2,2,896]{3,2,1,0:T(2,128)(2,1)}), bf16[8,2,2,896]{3,2,1,0:T(2,128)(2,1)S(1)}, u32[]{:S(2)}, u32[]{:S(2)}) async-start(bf16[8,2,2,896]{3,2,1,0:T(2,128)(2,1)} %pad_maximum_fusion.3), calls=%async_computation.1 | async-start | bytes 114688 | tf_op jit(solution)/shard_map/all_to_all | solution.py:152
  100.1 9.2 %all-to-all-start.3 = ((bf16[8,2,2,896]{3,2,1,0:T(2,128)(2,1)}), bf16[8,2,2,896]{3,2,1,0:T(2,128)(2,1)S(1)}, u32[]{:S(2)}, u32[]{:S(2)}) async-start(bf16[8,2,2,896]{3,2,1,0:T(2,128)(2,1)} %pad_maximum_fusion.4), calls=%async_computation.3 | async-start | bytes 114688 | tf_op jit(solution)/shard_map/all_to_all | solution.py:153
Sparse Core Ops, SparseCore 0:
  35.1 43.6 all-reduce.1
